TPU v7x, 32 devices: a whole 2x2x4 slice. The times are simulated.
32 devices in a mesh: tm: 8 (over y, x, core), space: 4 (over z).
Axes of the slice: x: 2, y: 2, z: 4, core: 2. Of those that a mesh axis runs over, the one named last changes fastest.
Arguments:
- panel: bfloat16 [8, 32, 2, 3, 4, 512], P('tm', None, None, None, 'space'), may hold values from -0.25 to 0.25
- gauge: bfloat16 [8, 4, 2, 3, 3, 4, 512], P('tm', None, None, None, None, 'space'), may hold values from -2.390625 to 2.390625
- momenta: int32 [8, 3], replicated, may hold values from -2 to 2
- op_momentum: int32 [8], replicated, may hold values from 0 to 7
- op_displacement: int32 [8], replicated, may hold values from 0 to 3
Outputs:
- elementals: float32 [8, 8, 2, 32, 32], P('space', 'tm')
All inputs are finite; a program needn't handle non-finite values.
Results may differ from a plain program's by a relative error of at most 0.0038.
Values may be sent and summed in bfloat16 or wider, within the bound.
A program may use at most 64 MiB of HBM per device.

v0:
```python
import math

import jax
import jax.numpy as jnp
from jax import lax
from jax.sharding import PartitionSpec as P

LY = 16
LZ = 32


def shifted(x, axis, by):
    devices = lax.axis_size(axis)
    return lax.ppermute(x, axis, [(i, (i + by) % devices) for i in range(devices)])


def padded(cells, sides, width):
    for axis, dim in sides:
        count = lax.axis_size(axis)
        head = lax.slice_in_dim(cells, 0, width, axis=dim)
        tail = lax.slice_in_dim(cells, cells.shape[dim] - width, cells.shape[dim], axis=dim)
        cells = jnp.concatenate(
            [
                lax.ppermute(tail, axis, [(i, (i + 1) % count) for i in range(count)]),
                cells,
                lax.ppermute(head, axis, [((i + 1) % count, i) for i in range(count)]),
            ],
            axis=dim,
        )
    return cells


def link_times(gauge_link, source, adjoint):
    real_link = gauge_link[0]
    imag_link = gauge_link[1]
    if adjoint:
        real_link = jnp.swapaxes(real_link, 0, 1)
        imag_link = -jnp.swapaxes(imag_link, 0, 1)
    source_real = source[:, 0][:, None]
    source_imag = source[:, 1][:, None]
    out_real = jnp.sum(real_link[None] * source_real - imag_link[None] * source_imag, axis=2)
    out_imag = jnp.sum(real_link[None] * source_imag + imag_link[None] * source_real, axis=2)
    return jnp.stack([out_real, out_imag], axis=1)


def neighbour(source, direction, offset):
    if direction == 1:
        return jnp.roll(source, -offset * LZ, axis=-1)
    field_shape = source.shape
    site_grid = source.reshape(field_shape[:-1] + (LY, LZ))
    return jnp.roll(site_grid, -offset, axis=-1).reshape(field_shape)


def phases(momentum_row, coord_x, coord_y, coord_z, extent_x):
    part_x = jnp.mod(momentum_row[0] * coord_x, extent_x).astype(jnp.float32) / extent_x
    part_y = jnp.mod(momentum_row[1] * coord_y, LY).astype(jnp.float32) / LY
    part_z = jnp.mod(momentum_row[2] * coord_z, LZ).astype(jnp.float32) / LZ
    angle_total = 2.0 * math.pi * (part_x[:, None] + (part_y + part_z)[None, :])
    return (jnp.cos(angle_total), jnp.sin(angle_total))


def rotate(source, cosine, sine_part):
    real_part = source[:, 0]
    imag_part = source[:, 1]
    return jnp.stack(
        [cosine * real_part - sine_part * imag_part, cosine * imag_part + sine_part * real_part],
        axis=1,
    ).astype(jnp.bfloat16)


def contract(left_rows, right_rows):
    row_total = left_rows.shape[0]
    halves = left_rows.reshape(row_total, 2, -1)
    stacked = jnp.concatenate(
        [halves.reshape(row_total, -1), jnp.concatenate([-halves[:, 1], halves[:, 0]], axis=1)],
        axis=0,
    )
    flat_right = right_rows.reshape(right_rows.shape[0], -1)
    return jnp.dot(stacked, flat_right.T, preferred_element_type=jnp.float32)


def conj_transpose(matrix):
    vectors = matrix.shape[-1]
    real_part = matrix[..., :vectors, :]
    imag_part = matrix[..., vectors:, :]
    return jnp.concatenate(
        [jnp.swapaxes(real_part, -1, -2), -jnp.swapaxes(imag_part, -1, -2)], axis=-2
    )


def spatial_hops(current, wide_plane, gauge_here, lower_plane):
    forward = link_times(gauge_here[0], wide_plane[:, :, :, 2:], False)
    backward = link_times(lower_plane, wide_plane[:, :, :, :-2], True)
    hop_list = [(forward - backward).astype(jnp.bfloat16)]
    for direction in (1, 2):
        forward = link_times(gauge_here[direction], neighbour(current, direction, 1), False)
        lower_link = neighbour(gauge_here[direction], direction, -1)
        backward = link_times(lower_link, neighbour(current, direction, -1), True)
        hop_list.append((forward - backward).astype(jnp.bfloat16))
    return hop_list


def shards(panel, gauge, momenta, op_momentum, op_displacement):
    slices = panel.shape[0]
    vectors = panel.shape[1]
    planes = panel.shape[4]
    site_count = panel.shape[5]
    moment_count = momenta.shape[0]
    space_rank = lax.axis_index("space")
    extent_x = planes * lax.axis_size("space")
    coord_x = space_rank * planes + jnp.arange(planes, dtype=jnp.int32)
    site_index = jnp.arange(site_count, dtype=jnp.int32)
    coord_y = site_index // LZ
    coord_z = site_index % LZ
    ahead_slice = shifted(panel, "tm", -1)
    upcoming = jnp.concatenate([panel[1:], ahead_slice], axis=0)
    wide_x = padded(panel, (("space", 4),), 1)
    lower_plane = shifted(gauge[:, 0, :, :, :, planes - 1 :], "space", 1)
    links_x = jnp.concatenate([lower_plane, gauge[:, 0]], axis=4)
    current = panel[0].astype(jnp.float32)
    gauge_here = gauge[0].astype(jnp.float32)
    hop_list = spatial_hops(
        current,
        wide_x[0].astype(jnp.float32),
        gauge_here,
        links_x[0, :, :, :, :-1].astype(jnp.float32),
    )
    time_hop = link_times(gauge_here[3], upcoming[0].astype(jnp.float32), False).astype(
        jnp.bfloat16
    )
    right_all = jnp.concatenate(hop_list + [time_hop], axis=0)

    def per_moment(moment):
        cosine, sine_part = phases(momenta[moment], coord_x, coord_y, coord_z, extent_x)
        main_part = contract(rotate(current, cosine, sine_part), right_all)
        back_phase = rotate(current, cosine, -sine_part)
        extra_part = contract(back_phase, time_hop)
        return (main_part, extra_part)

    main_part, extra_part = lax.map(per_moment, jnp.arange(moment_count, dtype=jnp.int32))
    main_list = [main_part]
    extra_list = [extra_part]
    main_terms = jnp.stack(main_list, axis=0)
    extra_terms = jnp.stack(extra_list, axis=0)
    carried = shifted(extra_terms, "tm", 1)
    back_terms = conj_transpose(jnp.concatenate([carried, extra_terms[:-1]], axis=0))
    elemental_table = main_terms.reshape(slices, moment_count, 2 * vectors, 4, vectors).transpose(
        0, 1, 3, 2, 4
    )
    elemental_table = jnp.concatenate(
        [elemental_table[:, :, :3], (elemental_table[:, :, 3] - back_terms)[:, :, None]], axis=2
    )
    table_flat = elemental_table.transpose(1, 2, 0, 3, 4).reshape(moment_count * 4, -1)
    combined = op_momentum * 4 + op_displacement
    table_ids = jnp.arange(moment_count * 4, dtype=jnp.int32)
    rows_here = op_momentum.shape[0] // lax.axis_size("space")
    onehot = (combined[:, None] == table_ids[None, :]).astype(jnp.float32)
    summed = lax.psum_scatter(
        jnp.dot(onehot, table_flat, precision=lax.Precision.HIGHEST),
        "space",
        scatter_dimension=0,
        tiled=True,
    )
    return summed.reshape(rows_here, slices, 2, vectors, vectors)


def solution(mesh):
    placed = (
        P("tm", None, None, None, "space", None),
        P("tm", None, None, None, None, "space", None),
        P(),
        P(),
        P(),
    )
    return jax.shard_map(
        shards,
        mesh=mesh,
        in_specs=placed,
        out_specs=P("space", "tm", None, None, None),
        check_vma=False,
    )
```

profile of v0, /device:TPU:0, one launch (start us, length us, event | category | flops | bytes accessed | tf_op | source)
XLA Modules:
  0.0 157.0 jit_solution(5657613464542543231)
XLA Ops:
  6.5 1.6 %copy.87 = bf16[1,32,2,3,1,512]{5,1,4,3,2,0:T(8,128)(2,1)} copy(bf16[1,32,2,3,1,512]{5,2,4,3,1,0:T(2,128)(2,1)} %param.7) | data formatting | bytes 393216 | tf_op args[0]
  8.2 3.1 %collective-permute-start = (bf16[1,32,2,3,1,512]{5,1,4,3,2,0:T(8,128)(2,1)}, bf16[1,32,2,3,1,512]{5,1,4,3,2,0:T(8,128)(2,1)}, u32[]{:S(2)}, u32[]{:S(2)}) collective-permute-start(bf16[1,32,2,3,1,512]{5,1,4,3,2,0:T(8,128)(2,1)} %copy.87), channel_id=1, source_target_pairs={{0,1},{1,2},{2,3},{3,0},{4,5},{5,6},{6,7},{7,4},{8,9},{9,10},{10,1... | collective-permute-start | bytes 589832 | tf_op jit(solution)/shard_map/ppermute | solution.py:24
  11.2 2.0 %collective-permute-start.1 = (bf16[1,32,2,3,1,512]{5,1,4,3,2,0:T(8,128)(2,1)}, bf16[1,32,2,3,1,512]{5,1,4,3,2,0:T(8,128)(2,1)}, u32[]{:S(2)}, u32[]{:S(2)}) collective-permute-start(bf16[1,32,2,3,1,512]{5,1,4,3,2,0:T(8,128)(2,1)} %copy.87), channel_id=1, source_target_pairs={{1,0},{2,1},{3,2},{0,3},{5,4},{6,5},{7,6},{4,7},{9,8},{10,9},{11,1... | collective-permute-start | bytes 589832 | tf_op jit(solution)/shard_map/ppermute | solution.py:26
  13.2 1.3 slice_bitcast_fusion.13
  14.6 1.8 %copy_convert_fusion = (f32[1,32,2,3,1,512]{5,1,3,2,4,0:T(8,128)S(1)}, f32[32,2,3,1,512]{4,0,3,2,1:T(8,128)S(1)}, bf16[1,32,2,3,1,512]{5,1,3,2,4,0:T(8,128)(2,1)}) fusion(bf16[1,32,2,3,1,512]{5,2,4,3,1,0:T(2,128)(2,1)} %param.7), kind=kLoop, calls=%fused_computation.150 | loop fusion | flops 98304 | bytes 1179648 | tf_op jit(solution)/shard_map/convert_element_type | solution.py:120
  16.4 1.6 %collective-permute-start.3 = (bf16[1,32,2,3,1,512]{5,1,3,2,4,0:T(8,128)(2,1)}, bf16[1,32,2,3,1,512]{5,1,3,2,4,0:T(8,128)(2,1)}, u32[]{:S(2)}, u32[]{:S(2)}) collective-permute-start(bf16[1,32,2,3,1,512]{5,1,3,2,4,0:T(8,128)(2,1)} %get-tuple-element.304), channel_id=1, source_target_pairs={{0,28},{4,0},{8,4},{12,8},{16,12},{20,16},{24,20},{28,24},{1,29},{... | collective-permute-start | bytes 589832 | tf_op jit(solution)/shard_map/ppermute | solution.py:14
  18.0 1.0 fusion.65
  19.0 0.7 fusion.64
  19.8 0.4 reshape.822
  20.2 0.5 fusion.62
  20.8 0.5 fusion.63
  21.3 0.6 slice.329
  21.9 0.8 fusion.66
  22.8 0.5 copy-done.6
  23.3 0.9 pad_maximum_fusion.2
  24.2 1.4 reshape.815
  25.5 1.0 slice_bitcast_fusion.5
  26.6 0.6 reshape.816
  29.9 0.7 convert_element_type.212
  30.7 1.2 fusion.39
  32.0 1.0 bitcast_convert_fusion
  33.7 0.4 copy.98
  34.5 0.4 copy-done.2
  35.0 71.1 %while.17 = (s32[]{:T(128)}, f32[8,64,128]{2,1,0:T(8,128)S(1)}, f32[8,64,32]{1,2,0:T(8,128)S(1)}, s32[8]{0:T(128)S(1)}, s32[8,3]{0,1:T(4,128)S(1)}, /*index=5*/s...) while((s32[]{:T(128)}, f32[8,64,128]{2,1,0:T(8,128)S(1)}, ...), condition=%wide.wide.region_15.16_spmd.clone, body=%wide.wide.region_14.15_spmd.clone.sunk | while | flops 66301456 | bytes 6359468 | solution.py:140
  35.0 0.6 dynamic_slice.23
  37.7 0.6 fusion.95
  38.9 1.4 fusion.97
  40.3 1.4 fusion.96
  43.8 0.7 dynamic_slice.23
  46.6 0.6 fusion.95
  47.8 1.4 fusion.97
  49.2 1.4 fusion.96
  52.7 0.7 dynamic_slice.23
  55.5 0.6 fusion.95
  56.7 1.4 fusion.97
  58.1 1.4 fusion.96
  61.6 0.7 dynamic_slice.23
  64.4 0.6 fusion.95
  65.5 1.4 fusion.97
  66.9 1.4 fusion.96
  70.5 0.7 dynamic_slice.23
  73.3 0.6 fusion.95
  74.4 1.4 fusion.97
  75.8 1.4 fusion.96
  79.4 0.7 dynamic_slice.23
  82.1 0.6 fusion.95
  83.3 1.4 fusion.97
  84.7 1.4 fusion.96
  88.3 0.7 dynamic_slice.23
  91.0 0.6 fusion.95
  92.2 1.4 fusion.97
  93.6 1.4 fusion.96
  97.2 0.7 dynamic_slice.23
  99.9 0.6 fusion.95
  101.1 1.4 fusion.97
  102.5 1.4 fusion.96
  106.5 6.4 %collective-permute-done.4 = f32[1,8,64,32]{3,2,1,0:T(8,128)S(1)} collective-permute-done((f32[1,8,64,32]{3,2,1,0:T(8,128)S(1)}, f32[1,8,64,32]{3,2,1,0:T(8,128)S(1)}, u32[]{:S(2)}, u32[]{:S(2)}) %collective-permute-start.4) | collective-permute-done | bytes 65568 | tf_op jit(solution)/shard_map/ppermute | solution.py:14
  113.1 0.4 copy.103
  113.5 0.5 reshape_transpose.3
  114.0 0.9 fusion.57
  114.9 0.6 dynamic-slice
  116.1 32.5 %all-reduce.3.cloned.1.call-done = f32[8,2048]{1,0:T(8,128)} async-done(((f32[8,2048]{1,0:T(8,128)}), f32[8,2048]{1,0:T(8,128)}) %all-reduce.3.cloned.1.call-update) | async-done | bytes 65552
  148.6 0.8 constant_dynamic-slice_fusion.1
  149.4 0.7 reshape.817
  (214 shorter events, 21.3 us)
Async XLA Ops:
  6.5 142.1 %all-reduce.3.cloned.1.call-start = ((), (), s32[]{:S(2)}) async-start(), calls=%async_computation | async-start | bytes 131072
  8.2 22.5 %collective-permute-start = (bf16[1,32,2,3,1,512]{5,1,4,3,2,0:T(8,128)(2,1)}, bf16[1,32,2,3,1,512]{5,1,4,3,2,0:T(8,128)(2,1)}, u32[]{:S(2)}, u32[]{:S(2)}) collective-permute-start(bf16[1,32,2,3,1,512]{5,1,4,3,2,0:T(8,128)(2,1)} %copy.87), channel_id=1, source_target_pairs={{0,1},{1,2},{2,3},{3,0},{4,5},{5,6},{6,7},{7,4},{8,9},{9,10},{10,1... | collective-permute-start | bytes 589832 | tf_op jit(solution)/shard_map/ppermute | solution.py:24
  11.2 19.5 %collective-permute-start.1 = (bf16[1,32,2,3,1,512]{5,1,4,3,2,0:T(8,128)(2,1)}, bf16[1,32,2,3,1,512]{5,1,4,3,2,0:T(8,128)(2,1)}, u32[]{:S(2)}, u32[]{:S(2)}) collective-permute-start(bf16[1,32,2,3,1,512]{5,1,4,3,2,0:T(8,128)(2,1)} %copy.87), channel_id=1, source_target_pairs={{1,0},{2,1},{3,2},{0,3},{5,4},{6,5},{7,6},{4,7},{9,8},{10,9},{11,1... | collective-permute-start | bytes 589832 | tf_op jit(solution)/shard_map/ppermute | solution.py:26
  14.6 5.1 %copy-start.5 = (bf16[1,4,2,3,3,1,512]{6,2,5,4,3,1,0:T(2,128)(2,1)S(1)}, bf16[1,4,2,3,3,1,512]{6,2,5,4,3,1,0:T(2,128)(2,1)}, u32[]{:S(2)}) copy-start(bf16[1,4,2,3,3,1,512]{6,2,5,4,3,1,0:T(2,128)(2,1)} %param.8) | copy-start | bytes 221188
  14.6 15.3 %collective-permute-start.2 = (bf16[1,2,3,3,1,512]{5,1,3,2,4,0:T(2,128)(2,1)}, bf16[1,2,3,3,1,512]{5,1,3,2,4,0:T(2,128)(2,1)}, u32[]{:S(2)}, u32[]{:S(2)}) collective-permute-start(bf16[1,2,3,3,1,512]{5,1,3,2,4,0:T(2,128)(2,1)} %slice_bitcast_fusion.13), channel_id=1, source_target_pairs={{0,1},{1,2},{2,3},{3,0},{4,5},{5,6},{6,7},{7,4},{8,9},{9,10},{10,1... | collective-permute-start | bytes 55304 | tf_op jit(solution)/shard_map/ppermute | solution.py:14
  16.4 15.6 %collective-permute-start.3 = (bf16[1,32,2,3,1,512]{5,1,3,2,4,0:T(8,128)(2,1)}, bf16[1,32,2,3,1,512]{5,1,3,2,4,0:T(8,128)(2,1)}, u32[]{:S(2)}, u32[]{:S(2)}) collective-permute-start(bf16[1,32,2,3,1,512]{5,1,3,2,4,0:T(8,128)(2,1)} %get-tuple-element.304), channel_id=1, source_target_pairs={{0,28},{4,0},{8,4},{12,8},{16,12},{20,16},{24,20},{28,24},{1,29},{... | collective-permute-start | bytes 589832 | tf_op jit(solution)/shard_map/ppermute | solution.py:14
  22.7 0.6 copy-start.6
  26.6 0.8 copy-start.8
  26.6 1.3 copy-start.15
  26.6 1.3 copy-start.16
  26.6 1.4 copy-start.7
  27.3 0.9 copy-start.13
  27.3 0.9 copy-start.14
  27.3 1.0 copy-start.11
  27.3 1.0 copy-start.12
  27.3 1.0 copy-start.9
  27.3 1.0 copy-start.10
  27.3 1.1 copy-start
  27.3 1.2 copy-start.1
  27.3 1.2 copy-start.3
  27.3 1.2 copy-start.4
  33.7 1.3 copy-start.17
  34.2 0.7 copy-start.2
  34.9 71.3 %copy-start.18 = (s32[8]{0:T(128)S(1)}, s32[8]{0:T(128)}, u32[]{:S(2)}) copy-start(s32[8]{0:T(128)} %param.11) | copy-start | bytes 100
  35.0 71.3 %copy-start.19 = (s32[8]{0:T(128)S(1)}, s32[8]{0:T(128)}, u32[]{:S(2)}) copy-start(s32[8]{0:T(128)} %param.10) | copy-start | bytes 100
  106.2 6.7 %collective-permute-start.4 = (f32[1,8,64,32]{3,2,1,0:T(8,128)S(1)}, f32[1,8,64,32]{3,2,1,0:T(8,128)S(1)}, u32[]{:S(2)}, u32[]{:S(2)}) collective-permute-start(f32[1,8,64,32]{3,2,1,0:T(8,128)S(1)} %bitcast.272), channel_id=1, source_target_pairs={{0,4},{4,8},{8,12},{12,16},{16,20},{20,24},{24,28},{28,0},{1,5},{5... | collective-permute-start | bytes 196616 | tf_op jit(solution)/shard_map/ppermute | solution.py:14
  113.1 1.8 %copy-start.20 = (u32[32]{0:T(128)S(1)}, u32[32]{0:T(128)}, u32[]{:S(2)}) copy-start(u32[32]{0:T(128)} %constant.162) | copy-start | bytes 388
Sparse Core Ops, SparseCore 0:
  115.0 33.5 all-reduce.2
where the time goes:
time: 158 us; the launch traced here: 157 us
  waiting for transfers between devices  38.9 us (25%)
  other arithmetic  36 us (23%)
  local copies, waits for them, and re-layouts  34.1 us (22%)
  loops' own time  21.8 us (14%)
  between operations  14.7 us (9%)
  starting transfers between devices  6.75 us (4%)
  matrix products  4.77 us (3%)
    unnamed x2, waiting for transfers between devices  32.5 us
    another operation x1, loops' own time, shards(): lax.map(per_moment, jnp.arange(moment_count, dtype=jnp.int32))  21.8 us
    neg x8, other arithmetic, per_moment(): back_phase = rotate(current, cosine, -sine_part)  11.3 us
    sin x8, other arithmetic, phases(): return (jnp.cos(angle_total), jnp.sin(angle_total))  11.2 us
    ppermute x3, waiting for transfers between devices, shifted(): lax.ppermute(x, axis, [(i, (i + by) % devices) for i in range(devices)])  6.41 us
    dynamic_slice x8, local copies, waits for them, and re-layouts, shards(): lax.map(per_moment, jnp.arange(moment_count, dtype=jnp.int32))  5.2 us
    unnamed x52, local copies, waits for them, and re-layouts  5.16 us
    slice x8, local copies, waits for them, and re-layouts, phases(): momentum_row[0] * coord_x  4.71 us
  transfers between devices with their start and end apart: 6, of which 2 were waited for; matrix products, arithmetic and copies ran while one was open for 11% of the time, Pallas kernels for 0%

commit v1 on v0

v1 whole, which is shorter than its diff:
```python
import functools
import math

import jax
import jax.numpy as jnp
from jax import lax
from jax.experimental import pallas as pl
from jax.experimental.pallas import tpu as pltpu
from jax.sharding import PartitionSpec as P

LY = 16
LZ = 32
F32 = jnp.float32
BF16 = jnp.bfloat16
COLOURS = 3
MESH = pl.DeviceIdType.MESH


def nt_dot(a, b):
    return lax.dot_general(a, b, (((1,), (1,)), ((), ())), preferred_element_type=F32)


def kernel(
    n_tm, n_space, v, g, mom, op_m, op_d, out,
    gf, gbf, cs, rot, back, hops, tmp, table, hx, ht, hb, gb, stage, got,
    send_sem, recv_sem,
):
    vectors, sites = v.shape[2], v.shape[3]
    moments = mom.shape[1]
    rows_here = out.shape[0]
    half = COLOURS * sites
    lanes = 128
    chunks = [slice(q * lanes, (q + 1) * lanes) for q in range(sites // lanes)]
    tm, space = lax.axis_index("tm"), lax.axis_index("space")
    tm_prev, tm_next = lax.rem(tm + n_tm - 1, n_tm), lax.rem(tm + 1, n_tm)
    space_prev = lax.rem(space + n_space - 1, n_space)

    barrier = pltpu.get_barrier_semaphore()
    for step in range(1, n_space):
        pl.semaphore_signal(
            barrier, inc=1, device_id=(tm, lax.rem(space + step, n_space)), device_id_type=MESH
        )
    for other in (tm_prev, tm_next):
        pl.semaphore_signal(barrier, inc=1, device_id=(other, space), device_id_type=MESH)
    pl.semaphore_wait(barrier, n_space + 1)

    def send(src, dst, index, device):
        copy = pltpu.make_async_remote_copy(
            src_ref=src, dst_ref=dst, send_sem=send_sem.at[index], recv_sem=recv_sem.at[index],
            device_id=device, device_id_type=MESH,
        )
        copy.start()
        return copy

    x_copies = [send(v.at[b], hx.at[b], b, (tm, space_prev)) for b in range(COLOURS)]
    t_copies = [
        send(v, ht, 3, (tm_prev, space)),
        send(v, hb, 4, (tm_next, space)),
        send(g.at[3], gb, 5, (tm_next, space)),
    ]

    gf[...] = g[...].astype(F32)

    def column(row):
        which = lax.broadcasted_iota(jnp.int32, (moments, sites), 0)
        value = jnp.zeros((moments, sites), jnp.int32)
        for m in range(moments):
            value = jnp.where(which == m, mom[row, m], value)
        return value

    site = lax.broadcasted_iota(jnp.int32, (moments, sites), 1)

    def part(momentum, coord, extent):
        turns = (momentum * coord).astype(F32) / extent
        return turns - jnp.floor(turns)

    px = column(0)
    part_yz = part(column(1), site // LZ, LY) + part(column(2), site % LZ, LZ)
    for shift in range(2):
        angle = (2.0 * math.pi) * (part(px, space + shift, n_space) + part_yz)
        for i, value in enumerate((jnp.cos(angle), jnp.sin(angle))):
            for m in range(moments):
                cs[2 * shift + i, m] = value[m : m + 1]

    def rotate(m, carry):
        rows = pl.ds(pl.multiple_of(m * vectors, vectors), vectors)
        for sl in chunks:
            c, s, cb, sb = (cs[i, m, :, sl] for i in range(4))
            for b in range(COLOURS):
                re = v[b, 0, :, sl].astype(F32)
                im = v[b, 1, :, sl].astype(F32)
                lo = slice(b * sites + sl.start, b * sites + sl.stop)
                hi = slice(half + lo.start, half + lo.stop)
                rot[rows, lo] = (c * re - s * im).astype(BF16)
                rot[rows, hi] = (c * im + s * re).astype(BF16)
                back[rows, lo] = (cb * re + sb * im).astype(BF16)
                back[rows, hi] = (cb * im - sb * re).astype(BF16)
        return carry

    lax.fori_loop(0, moments, rotate, 0)

    def link_row(links, mu, part_index, a, b, sl):
        row = part_index * COLOURS * COLOURS + a * COLOURS + b
        if mu is None:
            return links[row : row + 1, sl]
        return links[mu, row : row + 1, sl]

    def times(links, mu, source, sl, adjoint):
        src = [(source(b, 0, sl), source(b, 1, sl)) for b in range(COLOURS)]
        result = []
        for a in range(COLOURS):
            re = im = None
            for b in range(COLOURS):
                row, col = (b, a) if adjoint else (a, b)
                ur = link_row(links, mu, 0, row, col, sl)
                ui = link_row(links, mu, 1, row, col, sl)
                sr, si = src[b]
                if adjoint:
                    r, i = ur * sr + ui * si, ur * si - ui * sr
                else:
                    r, i = ur * sr - ui * si, ur * si + ui * sr
                re, im = (r, i) if re is None else (re + r, im + i)
            result.append((re, im))
        return result

    def put(d, a, sl, re, im):
        lo = slice(a * sites + sl.start, a * sites + sl.stop)
        hi = slice(half + lo.start, half + lo.stop)
        re, im = re.astype(BF16), im.astype(BF16)
        hops[d, :vectors, lo] = re
        hops[d, :vectors, hi] = im
        hops[d, vectors:, lo] = im
        hops[d, vectors:, hi] = -re

    in_z = lax.broadcasted_iota(jnp.int32, (vectors, sites), 1) % LZ

    def moved(value, direction, offset):
        if direction == 1:
            return pltpu.roll(value, (-offset * LZ) % sites, 1)
        near = pltpu.roll(value, -offset % sites, 1)
        wrap = pltpu.roll(value, (offset * (LZ - 1)) % sites, 1)
        edge = LZ - 1 if offset == 1 else 0
        return jnp.where(in_z == edge, wrap, near)

    def here(b, c, sl):
        return v[b, c, :, sl].astype(F32)

    whole = slice(0, sites)
    for d in (1, 2):
        for sl in chunks:
            for a, pair in enumerate(times(gf, d, here, sl, True)):
                for c in range(2):
                    tmp[1, a, c, :, sl] = pair[c]
        for a in range(COLOURS):
            for c in range(2):
                tmp[0, a, c] = moved(v[a, c].astype(F32), d, 1)
                tmp[1, a, c] = moved(tmp[1, a, c], d, -1)
        for sl in chunks:
            ahead = times(gf, d, lambda b, c, sl: tmp[0, b, c, :, sl], sl, False)
            for a, (re, im) in enumerate(ahead):
                put(d, a, sl, re - tmp[1, a, 0, :, sl], im - tmp[1, a, 1, :, sl])

    def fill(d):
        table[d] = nt_dot(rot[...], hops[d]).reshape(moments, vectors, 2 * vectors)

    fill(1)
    fill(2)

    for copy in t_copies:
        copy.wait()
    gbf[...] = gb[...].astype(F32)
    for sl in chunks:
        behind = times(gbf, None, lambda b, c, sl: hb[b, c, :, sl].astype(F32), sl, True)
        ahead = times(gf, 3, lambda b, c, sl: ht[b, c, :, sl].astype(F32), sl, False)
        for a in range(COLOURS):
            put(3, a, sl, ahead[a][0] - behind[a][0], ahead[a][1] - behind[a][1])
    fill(3)

    for copy in x_copies:
        copy.wait()
    for sl in chunks:
        ahead = times(gf, 0, lambda b, c, sl: hx[b, c, :, sl].astype(F32), sl, False)
        for a, (re, im) in enumerate(ahead):
            put(0, a, sl, re, im)
    mirror = nt_dot(hops[0], back[...])
    direct = nt_dot(rot[...], hops[0])
    for m in range(moments):
        cols = slice(m * vectors, (m + 1) * vectors)
        flipped = jnp.concatenate([mirror[:vectors, cols], -mirror[vectors:, cols]], axis=1)
        table[0, m] = direct[cols] - flipped

    sums = []
    for step in range(n_space):
        owner = lax.rem(space + step, n_space)
        for r in range(rows_here):
            k = owner * rows_here + r
            stage[step, :, r * 2 * vectors : (r + 1) * 2 * vectors] = table[op_d[k], op_m[k]]
        if step > 0:
            sums.append(send(stage.at[step], got.at[step - 1], 5 + step, (tm, owner)))
    total = stage[0]
    for step, copy in enumerate(sums):
        copy.wait()
        total = total + got[step]
    for r in range(rows_here):
        for c in range(2):
            start = (2 * r + c) * vectors
            out[r, c] = total[:, start : start + vectors]


def solution(mesh):
    n_tm, n_space = mesh.shape["tm"], mesh.shape["space"]

    def shards(panel, gauge, momenta, op_momentum, op_displacement):
        vectors, sites = panel.shape[1], panel.shape[5]
        moments = momenta.shape[0]
        rows_here = op_momentum.shape[0] // n_space
        links = 2 * COLOURS * COLOURS
        v = panel[0, :, :, :, 0].transpose(2, 1, 0, 3)
        g = gauge[0, :, :, :, :, 0].reshape(4, links, sites)
        wide = 2 * COLOURS * sites
        vmem = pl.BlockSpec(memory_space=pltpu.VMEM)
        smem = pl.BlockSpec(memory_space=pltpu.SMEM)
        out = pl.pallas_call(
            functools.partial(kernel, n_tm, n_space),
            out_shape=jax.ShapeDtypeStruct((rows_here, 2, vectors, vectors), F32),
            in_specs=[vmem, vmem, smem, smem, smem],
            out_specs=vmem,
            scratch_shapes=[
                pltpu.VMEM((4, links, sites), F32),
                pltpu.VMEM((links, sites), F32),
                pltpu.VMEM((4, moments, 1, sites), F32),
                pltpu.VMEM((moments * vectors, wide), BF16),
                pltpu.VMEM((moments * vectors, wide), BF16),
                pltpu.VMEM((4, 2 * vectors, wide), BF16),
                pltpu.VMEM((2, COLOURS, 2, vectors, sites), F32),
                pltpu.VMEM((4, moments, vectors, 2 * vectors), F32),
                pltpu.VMEM((COLOURS, 2, vectors, sites), BF16),
                pltpu.VMEM((COLOURS, 2, vectors, sites), BF16),
                pltpu.VMEM((COLOURS, 2, vectors, sites), BF16),
                pltpu.VMEM((links, sites), BF16),
                pltpu.VMEM((n_space, vectors, rows_here * 2 * vectors), F32),
                pltpu.VMEM((n_space - 1, vectors, rows_here * 2 * vectors), F32),
                pltpu.SemaphoreType.DMA((5 + n_space,)),
                pltpu.SemaphoreType.DMA((5 + n_space,)),
            ],
            compiler_params=pltpu.CompilerParams(collective_id=0, has_side_effects=True),
        )(v, g, momenta.T, op_momentum, op_displacement)
        return out[:, None]

    placed = (
        P("tm", None, None, None, "space", None),
        P("tm", None, None, None, None, "space", None),
        P(),
        P(),
        P(),
    )
    return jax.shard_map(
        shards,
        mesh=mesh,
        in_specs=placed,
        out_specs=P("space", "tm", None, None, None),
        check_vma=False,
    )
```

time: 158 us -> 23.7 us (0.15)
  waiting for transfers between devices: 38.9 us -> 0 us
  other arithmetic: 36 us -> 0 us
  local copies, waits for them, and re-layouts: 34.1 us -> 3.78 us
  loops' own time: 21.8 us -> 0 us
  Pallas kernels: 0 us -> 19.8 us
  between operations: 14.7 us -> 0.01 us
  starting transfers between devices: 6.75 us -> 0 us
  matrix products: 4.77 us -> 0 us
    unnamed x2 -> x0, waiting for transfers between devices: 32.5 us -> none
    another operation x1 -> x0, loops' own time: 21.8 us -> none  [shards(): lax.map(per_moment, jnp.arange(moment_count, dtype=jnp.int32))]
    pallas_call x0 -> x1, Pallas kernels: none -> 19.8 us  [shards(): pl.pallas_call(functools.partial(kernel, n_tm, n_space), out_shape=jax.Sh...]
    neg x16 -> x0, other arithmetic: 13 us -> none  [the longest x8 11.3 us: per_moment(): back_phase = rotate(current, cosine, -sine_part)]
    sin x8 -> x0, other arithmetic: 11.2 us -> none  [phases(): return (jnp.cos(angle_total), jnp.sin(angle_total))]
    slice x17 -> x0, local copies, waits for them, and re-layouts: 9.12 us -> none  [the longest x8 4.71 us: phases(): momentum_row[0] * coord_x]
    ppermute x5 -> x0, starting transfers between devices: 6.75 us -> none  [the longest x1 3.05 us: padded(): lax.ppermute(tail, axis, [(i, (i + 1) % count) for i in range(count)])]
    ppermute x5 -> x0, waiting for transfers between devices: 6.42 us -> none  [the longest x3 6.41 us: shifted(): lax.ppermute(x, axis, [(i, (i + by) % devices) for i in range(devices)])]
  transfers between devices with their start and end apart: 6 -> 0, of which waited for: 2 -> 0; matrix products, arithmetic and copies ran while one was open for 11% -> 0% of each run, Pallas kernels for 0% -> 0%
where the time goes in v1:
time: 23.7 us; the launch traced here: 23.6 us
  Pallas kernels  19.8 us (84%)
  local copies, waits for them, and re-layouts  3.78 us (16%)
    pallas_call x1, Pallas kernels, shards(): pl.pallas_call(functools.partial(kernel, n_tm, n_space), out_shape=jax.Sh...  19.8 us
    unnamed x5, local copies, waits for them, and re-layouts  3.13 us
    another operation x1, local copies, waits for them, and re-layouts, shards(): g = gauge[0, :, :, :, :, 0].reshape(4, links, sites)  0.65 us

profile of v1, /device:TPU:0, one launch (start us, length us, event | category | flops | bytes accessed | tf_op | source)
XLA Modules:
  0.0 23.6 jit_solution(11663511923837886864)
XLA Ops:
  0.0 0.0 copy-start
  0.0 1.0 %copy.10 = bf16[1,4,2,3,3,1,512]{6,1,4,3,2,5,0:T(4,128)(2,1)S(1)} copy(bf16[1,4,2,3,3,1,512]{6,2,5,4,3,1,0:T(2,128)(2,1)} %param.6) | data formatting | bytes 147456 | tf_op args[1]
  1.0 0.6 %copy.11.g = bf16[4,18,512]{2,1,0:T(8,128)(2,1)} copy(bf16[4,18,512]{2,0,1:T(4,128)(2,1)S(1)} %bitcast.11) | data formatting | bytes 147456 | tf_op jit(solution)/shard_map/reshape;squeeze | solution.py:219
  1.6 0.0 copy-done
  1.6 0.7 %copy.14 = bf16[1,32,2,3,1,512]{5,1,2,3,4,0:T(8,128)(2,1)} copy(bf16[1,32,2,3,1,512]{5,2,4,3,1,0:T(2,128)(2,1)S(1)} %copy-done) | data formatting | bytes 393216 | tf_op args[0]
  2.3 19.8 %shard_map.55 = f32[2,2,32,32]{3,2,1,0:T(8,128)} custom-call(bf16[3,2,32,512]{3,2,1,0:T(8,128)(2,1)} %bitcast.10, bf16[4,18,512]{2,1,0:T(8,128)(2,1)} %copy.11.g, s32[3,8]{1,0:T(4,128)} %bitcast.13, s32[8]{0:T(128)} %op_m.1, s32[8]{0:T(128)} %op_d.1), custom_call_target="tpu_custom_call" | custom-call | tf_op jit(solution)/shard_map/pallas_call | solution.py:223
  22.1 1.5 %copy.16 = f32[2,1,2,32,32]{4,3,2,1,0:T(8,128)} copy(f32[2,1,2,32,32]{4,3,2,1,0:T(8,128)} %bitcast.12) | data formatting | bytes 32768
Async XLA Ops:
  0.0 1.6 %copy-start = (bf16[1,32,2,3,1,512]{5,2,4,3,1,0:T(2,128)(2,1)S(1)}, bf16[1,32,2,3,1,512]{5,2,4,3,1,0:T(2,128)(2,1)}, u32[]{:S(2)}) copy-start(bf16[1,32,2,3,1,512]{5,2,4,3,1,0:T(2,128)(2,1)} %param.5) | copy-start | bytes 589828

commit v2 on v1

v2 whole, which is shorter than its diff:
```python
import functools
import math

import jax
import jax.numpy as jnp
from jax import lax
from jax.experimental import pallas as pl
from jax.experimental.pallas import tpu as pltpu
from jax.sharding import PartitionSpec as P

LY = 16
LZ = 32
F32 = jnp.float32
BF16 = jnp.bfloat16
COLOURS = 3
MESH = pl.DeviceIdType.MESH


def nt_dot(a, b):
    return lax.dot_general(a, b, (((1,), (1,)), ((), ())), preferred_element_type=F32)


def kernel(
    n_tm, n_space, panel, gauge, mom, op_m, op_d, out,
    raw, links, vf, gf, gbf, cs, rot, back, hops, tmp, table, hx, ht, hb, gb, stage, got,
    local_sem, send_sem, recv_sem,
):
    vectors, sites = raw.shape[0], raw.shape[3]
    moments = mom.shape[1]
    rows_here = out.shape[0]
    half = COLOURS * sites
    lanes = 128
    chunks = [slice(q * lanes, (q + 1) * lanes) for q in range(sites // lanes)]
    tm, space = lax.axis_index("tm"), lax.axis_index("space")
    tm_prev, tm_next = lax.rem(tm + n_tm - 1, n_tm), lax.rem(tm + 1, n_tm)
    space_prev = lax.rem(space + n_space - 1, n_space)

    barrier = pltpu.get_barrier_semaphore()
    for step in range(1, n_space):
        pl.semaphore_signal(
            barrier, inc=1, device_id=(tm, lax.rem(space + step, n_space)), device_id_type=MESH
        )
    for other in (tm_prev, tm_next):
        pl.semaphore_signal(barrier, inc=1, device_id=(other, space), device_id_type=MESH)
    loads = [
        pltpu.make_async_copy(panel, raw, local_sem.at[0]),
        pltpu.make_async_copy(gauge, links, local_sem.at[1]),
    ]
    for copy in loads:
        copy.start()
    pl.semaphore_wait(barrier, n_space + 1)

    def send(src, dst, index, device):
        copy = pltpu.make_async_remote_copy(
            src_ref=src, dst_ref=dst, send_sem=send_sem.at[index], recv_sem=recv_sem.at[index],
            device_id=device, device_id_type=MESH,
        )
        copy.start()
        return copy

    x_copies, t_copies = [], []
    for b in range(COLOURS):
        x_copies.append(send(panel.at[:, b], hx.at[:, b], b, (tm, space_prev)))
        t_copies.append([
            send(panel.at[:, b], ht.at[:, b], COLOURS + b, (tm_prev, space)),
            send(panel.at[:, b], hb.at[:, b], 2 * COLOURS + b, (tm_next, space)),
        ])
        if b == 0:
            t_copies[0].append(send(gauge.at[3], gb, 3 * COLOURS, (tm_next, space)))

    for copy in loads:
        copy.wait()
    gf[...] = links[...].astype(F32)
    for b in range(COLOURS):
        for c in range(2):
            vf[b, c] = raw[:, b, c].astype(F32)

    def column(row):
        which = lax.broadcasted_iota(jnp.int32, (moments, sites), 0)
        value = jnp.zeros((moments, sites), jnp.int32)
        for m in range(moments):
            value = jnp.where(which == m, mom[row, m], value)
        return value

    site = lax.broadcasted_iota(jnp.int32, (moments, sites), 1)

    def part(momentum, coord, extent):
        turns = (momentum * coord).astype(F32) / extent
        return turns - jnp.floor(turns)

    px = column(0)
    part_yz = part(column(1), site // LZ, LY) + part(column(2), site % LZ, LZ)
    for shift in range(2):
        angle = (2.0 * math.pi) * (part(px, space + shift, n_space) + part_yz)
        for i, value in enumerate((jnp.cos(angle), jnp.sin(angle))):
            for m in range(moments):
                cs[2 * shift + i, m] = value[m : m + 1]

    def rotate(m, carry):
        rows = pl.ds(pl.multiple_of(m * vectors, vectors), vectors)
        for sl in chunks:
            c, s, cb, sb = (cs[i, m, :, sl] for i in range(4))
            for b in range(COLOURS):
                re, im = vf[b, 0, :, sl], vf[b, 1, :, sl]
                lo = slice(b * sites + sl.start, b * sites + sl.stop)
                hi = slice(half + lo.start, half + lo.stop)
                rot[rows, lo] = (c * re - s * im).astype(BF16)
                rot[rows, hi] = (c * im + s * re).astype(BF16)
                back[rows, lo] = (cb * re + sb * im).astype(BF16)
                back[rows, hi] = (cb * im - sb * re).astype(BF16)
        return carry

    lax.fori_loop(0, moments, rotate, 0)

    def link_term(field, sr, si, a, b, sl, adjoint):
        at = (b, a) if adjoint else (a, b)
        ur, ui = (field[(*at, slice(c, c + 1), sl)] for c in range(2))
        if adjoint:
            return ur * sr + ui * si, ur * si - ui * sr
        return ur * sr - ui * si, ur * si + ui * sr

    def times(field, source, sl, adjoint):
        src = [(source[b, 0, :, sl], source[b, 1, :, sl]) for b in range(COLOURS)]
        result = []
        for a in range(COLOURS):
            terms = [link_term(field, *src[b], a, b, sl, adjoint) for b in range(COLOURS)]
            result.append(tuple(sum(t[c] for t in terms[1:]) + terms[0][c] for c in range(2)))
        return result

    def put(d, a, sl, re, im):
        lo = slice(a * sites + sl.start, a * sites + sl.stop)
        hi = slice(half + lo.start, half + lo.stop)
        re, im = re.astype(BF16), im.astype(BF16)
        hops[d, :vectors, lo] = re
        hops[d, :vectors, hi] = im
        hops[d, vectors:, lo] = im
        hops[d, vectors:, hi] = -re

    in_z = lax.broadcasted_iota(jnp.int32, (vectors, sites), 1) % LZ

    def moved(value, direction, offset):
        if direction == 1:
            return pltpu.roll(value, (-offset * LZ) % sites, 1)
        near = pltpu.roll(value, -offset % sites, 1)
        wrap = pltpu.roll(value, (offset * (LZ - 1)) % sites, 1)
        edge = LZ - 1 if offset == 1 else 0
        return jnp.where(in_z == edge, wrap, near)

    for d in (1, 2):
        for sl in chunks:
            for a, pair in enumerate(times(gf.at[d], vf, sl, True)):
                for c in range(2):
                    tmp[1, a, c, :, sl] = pair[c]
        for a in range(COLOURS):
            for c in range(2):
                tmp[0, a, c] = moved(vf[a, c], d, 1)
                tmp[1, a, c] = moved(tmp[1, a, c], d, -1)
        for sl in chunks:
            for a, (re, im) in enumerate(times(gf.at[d], tmp.at[0], sl, False)):
                put(d, a, sl, re - tmp[1, a, 0, :, sl], im - tmp[1, a, 1, :, sl])

    def fill(d):
        table[d] = nt_dot(rot[...], hops[d]).reshape(moments, vectors, 2 * vectors)

    fill(1)
    fill(2)

    def arrive(d, b):
        for sl in chunks:
            total = [[None] * 2 for _ in range(COLOURS)]
            parts = [(gf.at[0], hx, False)] if d == 0 else [(gf.at[3], ht, False), (gbf, hb, True)]
            for field, held, adjoint in parts:
                sr, si = (held[:, b, c, sl].astype(F32) for c in range(2))
                for a in range(COLOURS):
                    pair = link_term(field, sr, si, a, b, sl, adjoint)
                    for c in range(2):
                        value = pair[c]
                        if total[a][c] is not None:
                            value = total[a][c] - value
                        total[a][c] = value
            slot = 0 if d == 0 else 1
            for a in range(COLOURS):
                if b > 0:
                    total[a] = [tmp[slot, a, c, :, sl] + total[a][c] for c in range(2)]
                if b < COLOURS - 1:
                    for c in range(2):
                        tmp[slot, a, c, :, sl] = total[a][c]
                else:
                    put(d, a, sl, *total[a])

    for b in range(COLOURS):
        x_copies[b].wait()
        arrive(0, b)
        if b == COLOURS - 1:
            mirror = nt_dot(hops[0], back[...])
            direct = nt_dot(rot[...], hops[0])
            for m in range(moments):
                cols = slice(m * vectors, (m + 1) * vectors)
                flipped = jnp.concatenate([mirror[:vectors, cols], -mirror[vectors:, cols]], axis=1)
                table[0, m] = direct[cols] - flipped
        for copy in t_copies[b]:
            copy.wait()
        if b == 0:
            gbf[...] = gb[...].astype(F32)
        arrive(3, b)
    fill(3)

    sums = []
    for step in range(n_space):
        owner = lax.rem(space + step, n_space)
        for r in range(rows_here):
            k = owner * rows_here + r
            stage[step, :, r * 2 * vectors : (r + 1) * 2 * vectors] = table[op_d[k], op_m[k]]
        if step > 0:
            sums.append(send(stage.at[step], got.at[step - 1], 3 * COLOURS + step, (tm, owner)))
    total = stage[0]
    for step, copy in enumerate(sums):
        copy.wait()
        total = total + got[step]
    for r in range(rows_here):
        for c in range(2):
            start = (2 * r + c) * vectors
            out[r, c] = total[:, start : start + vectors]


def solution(mesh):
    n_tm, n_space = mesh.shape["tm"], mesh.shape["space"]

    def shards(panel, gauge, momenta, op_momentum, op_displacement):
        vectors, sites = panel.shape[1], panel.shape[5]
        moments = momenta.shape[0]
        rows_here = op_momentum.shape[0] // n_space
        v = panel[0, :, :, :, 0].transpose(0, 2, 1, 3)
        g = gauge[0, :, :, :, :, 0].transpose(0, 2, 3, 1, 4)
        wide = 2 * COLOURS * sites
        vmem = pl.BlockSpec(memory_space=pltpu.VMEM)
        smem = pl.BlockSpec(memory_space=pltpu.SMEM)
        hbm = pl.BlockSpec(memory_space=pl.ANY)
        sends = 3 * COLOURS + n_space
        out = pl.pallas_call(
            functools.partial(kernel, n_tm, n_space),
            out_shape=jax.ShapeDtypeStruct((rows_here, 2, vectors, vectors), F32),
            in_specs=[hbm, hbm, smem, smem, smem],
            out_specs=vmem,
            scratch_shapes=[
                pltpu.VMEM(v.shape, BF16),
                pltpu.VMEM(g.shape, BF16),
                pltpu.VMEM((COLOURS, 2, vectors, sites), F32),
                pltpu.VMEM(g.shape, F32),
                pltpu.VMEM(g.shape[1:], F32),
                pltpu.VMEM((4, moments, 1, sites), F32),
                pltpu.VMEM((moments * vectors, wide), BF16),
                pltpu.VMEM((moments * vectors, wide), BF16),
                pltpu.VMEM((4, 2 * vectors, wide), BF16),
                pltpu.VMEM((2, COLOURS, 2, vectors, sites), F32),
                pltpu.VMEM((4, moments, vectors, 2 * vectors), F32),
                pltpu.VMEM(v.shape, BF16),
                pltpu.VMEM(v.shape, BF16),
                pltpu.VMEM(v.shape, BF16),
                pltpu.VMEM(g.shape[1:], BF16),
                pltpu.VMEM((n_space, vectors, rows_here * 2 * vectors), F32),
                pltpu.VMEM((n_space - 1, vectors, rows_here * 2 * vectors), F32),
                pltpu.SemaphoreType.DMA((2,)),
                pltpu.SemaphoreType.DMA((sends,)),
                pltpu.SemaphoreType.DMA((sends,)),
            ],
            compiler_params=pltpu.CompilerParams(collective_id=0, has_side_effects=True),
        )(v, g, momenta.T, op_momentum, op_displacement)
        return out[:, None]

    placed = (
        P("tm", None, None, None, "space", None),
        P("tm", None, None, None, None, "space", None),
        P(),
        P(),
        P(),
    )
    return jax.shard_map(
        shards,
        mesh=mesh,
        in_specs=placed,
        out_specs=P("space", "tm", None, None, None),
        check_vma=False,
    )
```

time: 23.7 us -> 21.4 us (0.903)
  local copies, waits for them, and re-layouts: 3.78 us -> 1.47 us
    unnamed x5 -> x1, local copies, waits for them, and re-layouts: 3.13 us -> 1.47 us
    another operation x1 -> x0, local copies, waits for them, and re-layouts: 0.65 us -> none  [shards(): g = gauge[0, :, :, :, :, 0].reshape(4, links, sites)]
where the time goes in v2:
time: 21.4 us; the launch traced here: 21.2 us
  Pallas kernels  19.7 us (92%)
  local copies, waits for them, and re-layouts  1.47 us (7%)
    pallas_call x1, Pallas kernels, shards(): pl.pallas_call(functools.partial(kernel, n_tm, n_space), out_shape=jax.Sh...  19.7 us
    unnamed x1, local copies, waits for them, and re-layouts  1.47 us

profile of v2, /device:TPU:0, one launch (start us, length us, event | category | flops | bytes accessed | tf_op | source)
XLA Modules:
  0.0 21.2 jit_solution(2545402375030886850)
XLA Ops:
  0.0 19.7 %shard_map.55 = f32[2,2,32,32]{3,2,1,0:T(8,128)} custom-call(bf16[32,3,2,512]{3,2,1,0:T(2,128)(2,1)} %bitcast.11, bf16[4,3,3,2,512]{4,3,2,1,0:T(2,128)(2,1)} %bitcast.12, s32[3,8]{1,0:T(4,128)} %bitcast.13, s32[8]{0:T(128)} %op_m.1, s32[8]{0:T(128)} %op_d.1), custom_call_target="tpu_custom_call" | custom-call | tf_op jit(solution)/shard_map/pallas_call | solution.py:240
  19.7 1.5 %copy.8 = f32[2,1,2,32,32]{4,3,2,1,0:T(8,128)} copy(f32[2,1,2,32,32]{4,3,2,1,0:T(8,128)} %bitcast.10) | data formatting | bytes 32768

commit v3 on v2

--- a/solution.py
+++ b/solution.py
@@ -22,12 +22,12 @@
 
 def kernel(
     n_tm, n_space, panel, gauge, mom, op_m, op_d, out,
-    raw, links, vf, gf, gbf, cs, rot, back, hops, tmp, table, hx, ht, hb, gb, stage, got,
+    raw, links, vf, gf, gbf, cs, rot, back, hops, tmp, table, hx, ht, hb, gb, mine, stage, got,
     local_sem, send_sem, recv_sem,
 ):
     vectors, sites = raw.shape[0], raw.shape[3]
     moments = mom.shape[1]
-    rows_here = out.shape[0]
+    rows_here = out.shape[1] // (2 * vectors)
     half = COLOURS * sites
     lanes = 128
     chunks = [slice(q * lanes, (q + 1) * lanes) for q in range(sites // lanes)]
@@ -48,7 +48,6 @@
     ]
     for copy in loads:
         copy.start()
-    pl.semaphore_wait(barrier, n_space + 1)
 
     def send(src, dst, index, device):
         copy = pltpu.make_async_remote_copy(
@@ -58,6 +57,35 @@
         copy.start()
         return copy
 
+    for copy in loads:
+        copy.wait()
+    gf[...] = links[...].astype(F32)
+    for b in range(COLOURS):
+        for c in range(2):
+            vf[b, c] = raw[:, b, c].astype(F32)
+
+    def column(row):
+        which = lax.broadcasted_iota(jnp.int32, (moments, sites), 0)
+        value = jnp.zeros((moments, sites), jnp.int32)
+        for m in range(moments):
+            value = jnp.where(which == m, mom[row, m], value)
+        return value
+
+    site = lax.broadcasted_iota(jnp.int32, (moments, sites), 1)
+
+    def part(momentum, coord, extent):
+        turns = (momentum * coord).astype(F32) / extent
+        return turns - jnp.floor(turns)
+
+    px = column(0)
+    part_yz = part(column(1), site // LZ, LY) + part(column(2), site % LZ, LZ)
+    for shift in range(2):
+        angle = (2.0 * math.pi) * (part(px, space + shift, n_space) + part_yz)
+        for i, value in enumerate((jnp.cos(angle), jnp.sin(angle))):
+            for m in range(moments):
+                cs[2 * shift + i, m] = value[m : m + 1]
+
+    pl.semaphore_wait(barrier, n_space + 1)
     x_copies, t_copies = [], []
     for b in range(COLOURS):
         x_copies.append(send(panel.at[:, b], hx.at[:, b], b, (tm, space_prev)))
@@ -67,34 +95,6 @@
         ])
         if b == 0:
             t_copies[0].append(send(gauge.at[3], gb, 3 * COLOURS, (tm_next, space)))
-
-    for copy in loads:
-        copy.wait()
-    gf[...] = links[...].astype(F32)
-    for b in range(COLOURS):
-        for c in range(2):
-            vf[b, c] = raw[:, b, c].astype(F32)
-
-    def column(row):
-        which = lax.broadcasted_iota(jnp.int32, (moments, sites), 0)
-        value = jnp.zeros((moments, sites), jnp.int32)
-        for m in range(moments):
-            value = jnp.where(which == m, mom[row, m], value)
-        return value
-
-    site = lax.broadcasted_iota(jnp.int32, (moments, sites), 1)
-
-    def part(momentum, coord, extent):
-        turns = (momentum * coord).astype(F32) / extent
-        return turns - jnp.floor(turns)
-
-    px = column(0)
-    part_yz = part(column(1), site // LZ, LY) + part(column(2), site % LZ, LZ)
-    for shift in range(2):
-        angle = (2.0 * math.pi) * (part(px, space + shift, n_space) + part_yz)
-        for i, value in enumerate((jnp.cos(angle), jnp.sin(angle))):
-            for m in range(moments):
-                cs[2 * shift + i, m] = value[m : m + 1]
 
     def rotate(m, carry):
         rows = pl.ds(pl.multiple_of(m * vectors, vectors), vectors)
@@ -210,17 +210,19 @@
         owner = lax.rem(space + step, n_space)
         for r in range(rows_here):
             k = owner * rows_here + r
-            stage[step, :, r * 2 * vectors : (r + 1) * 2 * vectors] = table[op_d[k], op_m[k]]
+            picked = table[op_d[k], op_m[k]]
+            cols = slice(r * 2 * vectors, (r + 1) * 2 * vectors)
+            if step == 0:
+                mine[:, cols] = picked
+            else:
+                stage[step - 1, :, cols] = picked.astype(BF16)
         if step > 0:
-            sums.append(send(stage.at[step], got.at[step - 1], 3 * COLOURS + step, (tm, owner)))
-    total = stage[0]
+            sums.append(send(stage.at[step - 1], got.at[step - 1], 3 * COLOURS + step, (tm, owner)))
+    total = mine[...]
     for step, copy in enumerate(sums):
         copy.wait()
-        total = total + got[step]
-    for r in range(rows_here):
-        for c in range(2):
-            start = (2 * r + c) * vectors
-            out[r, c] = total[:, start : start + vectors]
+        total = total + got[step].astype(F32)
+    out[...] = total
 
 
 def solution(mesh):
@@ -239,7 +241,7 @@
         sends = 3 * COLOURS + n_space
         out = pl.pallas_call(
             functools.partial(kernel, n_tm, n_space),
-            out_shape=jax.ShapeDtypeStruct((rows_here, 2, vectors, vectors), F32),
+            out_shape=jax.ShapeDtypeStruct((vectors, rows_here * 2 * vectors), F32),
             in_specs=[hbm, hbm, smem, smem, smem],
             out_specs=vmem,
             scratch_shapes=[
@@ -258,15 +260,16 @@
                 pltpu.VMEM(v.shape, BF16),
                 pltpu.VMEM(v.shape, BF16),
                 pltpu.VMEM(g.shape[1:], BF16),
-                pltpu.VMEM((n_space, vectors, rows_here * 2 * vectors), F32),
-                pltpu.VMEM((n_space - 1, vectors, rows_here * 2 * vectors), F32),
+                pltpu.VMEM((vectors, rows_here * 2 * vectors), F32),
+                pltpu.VMEM((n_space - 1, vectors, rows_here * 2 * vectors), BF16),
+                pltpu.VMEM((n_space - 1, vectors, rows_here * 2 * vectors), BF16),
                 pltpu.SemaphoreType.DMA((2,)),
                 pltpu.SemaphoreType.DMA((sends,)),
                 pltpu.SemaphoreType.DMA((sends,)),
             ],
             compiler_params=pltpu.CompilerParams(collective_id=0, has_side_effects=True),
         )(v, g, momenta.T, op_momentum, op_displacement)
-        return out[:, None]
+        return out.reshape(vectors, rows_here, 2, vectors).transpose(1, 2, 0, 3)[:, None]
 
     placed = (
         P("tm", None, None, None, "space", None),

time: 21.4 us -> 21.3 us (level)
    unnamed x1 -> x0, local copies, waits for them, and re-layouts: 1.47 us -> none
    reshape x0 -> x2, local copies, waits for them, and re-layouts: none -> 1.46 us  [shards(): out.reshape(vectors, rows_here, 2, vectors).transpose(1, 2, 0, 3)[:, None]]
where the time goes in v3:
time: 21.3 us; the launch traced here: 21 us
  Pallas kernels  19.5 us (92%)
  local copies, waits for them, and re-layouts  1.46 us (7%)
    pallas_call x1, Pallas kernels, shards(): pl.pallas_call(functools.partial(kernel, n_tm, n_space), out_shape=jax.Sh...  19.5 us
    reshape x2, local copies, waits for them, and re-layouts, shards(): out.reshape(vectors, rows_here, 2, vectors).transpose(1, 2, 0, 3)[:, None]  1.46 us

profile of v3, /device:TPU:0, one launch (start us, length us, event | category | flops | bytes accessed | tf_op | source)
XLA Modules:
  0.0 21.0 jit_solution(3064516912679184914)
XLA Ops:
  0.0 19.5 %shard_map.55 = f32[32,128]{1,0:T(8,128)} custom-call(bf16[32,3,2,512]{3,2,1,0:T(2,128)(2,1)} %bitcast.12, bf16[4,3,3,2,512]{4,3,2,1,0:T(2,128)(2,1)} %bitcast.13, s32[3,8]{1,0:T(4,128)} %bitcast.14, s32[8]{0:T(128)} %op_m.1, s32[8]{0:T(128)} %op_d.1), custom_call_target="tpu_custom_call" | custom-call | tf_op jit(solution)/shard_map/pallas_call | solution.py:242
  19.5 0.8 %reshape.3 = f32[32,2,2,32]{3,2,1,0:T(2,128)S(1)} reshape(f32[32,128]{1,0:T(8,128)} %shard_map.55) | data formatting | bytes 32768 | tf_op jit(solution)/shard_map/reshape | solution.py:272
  20.4 0.6 %copy.8 = f32[32,2,2,32]{3,0,2,1:T(8,128)} copy(f32[32,2,2,32]{3,2,1,0:T(2,128)S(1)} %reshape.3) | data formatting | bytes 32768 | tf_op jit(solution)/shard_map/reshape | solution.py:272
